TPU v7x, 32 devices: a whole 2x2x4 slice. The times are simulated.
32 devices in a mesh: tile: 4 (over x, core), tm: 8 (over z, y).
Axes of the slice: x: 2, y: 2, z: 4, core: 2. Of those that a mesh axis runs over, the one named last changes fastest.
Arguments:
- ocean_heat_anomaly: bfloat16 [256, 96, 1024], P('tm', 'tile'), may hold values from -6 to 6
- observation_reliability: bfloat16 [256, 96, 1024], P('tm', 'tile'), may hold values from 0.099609375 to 1
- swath_date_number: int32 [256], replicated, may hold values from 0 to 255, as said below
- marine_cell_flag: int32 [96, 1024], P('tile'), may hold values 0 or 1
Outputs:
- trend: float32 [256, 96, 1024], P('tm', 'tile')
Inputs may be any that keep to these rules, and one draw needn't show every extreme that they name: `swath_date_number`: every day appears exactly once; every index of tm holds the same number of granules of every block of 32 consecutive days, in no particular order.
All inputs are finite; a program needn't handle non-finite values. No bound on the sum of `marine_cell_flag` on one device may be relied on, other than what follows from the above.
Results may differ from a plain program's by a relative error of at most 0.0015.
Values may be sent and summed in bfloat16 or wider, within the bound.
No kernel may reach another device: no remote copies, remote signals or barrier semaphores. Data moves between devices by JAX's collectives and lax.ppermute only.
A program may use at most 128 MiB of HBM per device.

v0:
```python
import math
import jax
import jax.numpy as jnp
from jax import lax
from jax.sharding import PartitionSpec as P

DECAY = 0.999
UNIT = 256.0
RIDGE = 0.05


def extended(array, sides, width):
    for axis, dim in sides:
        devices, length = (lax.axis_size(axis), array.shape[dim])
        up = [(i, (i + 1) % devices) for i in range(devices - 1)]
        down = [(j, i) for i, j in up]
        last = lax.slice_in_dim(array, length - width, length, axis=dim)
        leading = lax.slice_in_dim(array, 0, width, axis=dim)
        before = lax.ppermute(last, axis, up)
        after = lax.ppermute(leading, axis, down)
        array = jnp.concatenate([before, array, after], axis=dim)
    return array


def shifted(state, length):
    zeroth, first, second, level_sum, slope_sum = state
    factor = jnp.exp(length * math.log(DECAY))
    offset = length / UNIT
    return (
        factor * zeroth,
        factor * (first + offset * zeroth),
        factor * (second + 2.0 * offset * first + offset * offset * zeroth),
        factor * level_sum,
        factor * (slope_sum + offset * level_sum),
    )


def combine(earlier, later):
    moved = shifted(earlier[:5], later[5])
    joined = tuple((moved[index] + later[index] for index in range(5)))
    return joined + (earlier[5] + later[5],)


def on_device(ocean_heat_anomaly, observation_reliability, swath_date_number, marine_cell_flag):
    ntm = lax.axis_size("tm")
    me_time = lax.axis_index("tm")
    dates_for_shard = ocean_heat_anomaly.shape[0]
    share = dates_for_shard // ntm
    ocean = marine_cell_flag.astype(jnp.float32)
    all_days = swath_date_number.reshape(ntm, dates_for_shard)
    sort_keys = (
        all_days // dates_for_shard * dates_for_shard
        + jnp.arange(dates_for_shard, dtype=jnp.int32)[None]
    )
    send_order = jnp.argsort(sort_keys, axis=1)
    sorted_days = jnp.take_along_axis(all_days, send_order, axis=1)
    shard_ranking_permutation = lax.dynamic_index_in_dim(send_order, me_time, 0, keepdims=False)
    arrived = lax.dynamic_index_in_dim(
        sorted_days.reshape(ntm, ntm, share), me_time, 1, keepdims=False
    )
    positions = arrived.reshape(dates_for_shard) - me_time * dates_for_shard
    lag = jnp.arange(dates_for_shard, dtype=jnp.int32)[:, None] - positions[None, :]
    lag_days = lag.astype(jnp.float32)
    kernel_zero = jnp.where(lag >= 0, jnp.exp(lag_days * math.log(DECAY)), jnp.float32(0.0))
    kernel_one = kernel_zero * (lag_days / UNIT)
    kernel_two = kernel_one * (lag_days / UNIT)
    weight_kernel = jnp.concatenate([kernel_zero, kernel_one, kernel_two], axis=0)
    weight_high = weight_kernel.astype(jnp.bfloat16)
    weight_low = (weight_kernel - weight_high.astype(jnp.float32)).astype(jnp.bfloat16)
    value_kernel = jnp.concatenate([kernel_zero, kernel_one], axis=0)
    ranked_anomaly_field = ocean_heat_anomaly[shard_ranking_permutation]
    sorted_quality = observation_reliability[shard_ranking_permutation]
    anomaly_slice = lax.all_to_all(
        ranked_anomaly_field, "tm", split_axis=0, concat_axis=0, tiled=True
    )
    reliability_slice = lax.all_to_all(
        sorted_quality, "tm", split_axis=0, concat_axis=0, tiled=True
    )
    pointwise_multiple = reliability_slice.astype(jnp.float32) * anomaly_slice.astype(jnp.float32)
    weight_terms = jnp.einsum(
        "ks,src->krc", weight_high, reliability_slice, preferred_element_type=jnp.float32
    ) + jnp.einsum("ks,src->krc", weight_low, reliability_slice, preferred_element_type=jnp.float32)
    value_terms = jnp.einsum(
        "ks,src->krc",
        value_kernel,
        pointwise_multiple,
        precision=lax.Precision.HIGH,
        preferred_element_type=jnp.float32,
    )
    local = (
        weight_terms[:dates_for_shard],
        weight_terms[dates_for_shard : 2 * dates_for_shard],
        weight_terms[2 * dates_for_shard :],
        value_terms[:dates_for_shard],
        value_terms[dates_for_shard:],
    )
    local = tuple((part * ocean[None] for part in local))
    totals = tuple((part[dates_for_shard - 1] for part in local)) + (jnp.float32(dates_for_shard),)
    stacked = (
        lax.all_gather(totals[0][None], "tm", axis=0, tiled=True),
        lax.all_gather(totals[1][None], "tm", axis=0, tiled=True),
        lax.all_gather(totals[2][None], "tm", axis=0, tiled=True),
        lax.all_gather(totals[3][None], "tm", axis=0, tiled=True),
        lax.all_gather(totals[4][None], "tm", axis=0, tiled=True),
    )
    empty = jnp.zeros(ocean.shape, jnp.float32)

    def fold_block(index, state):
        element = tuple(
            (lax.dynamic_index_in_dim(part, index, 0, keepdims=False) for part in stacked)
        )
        merged = combine(state, element + (jnp.float32(dates_for_shard),))
        return tuple((jnp.where(index < me_time, new, old) for new, old in zip(merged, state)))

    carried = lax.fori_loop(
        0, ntm, fold_block, (empty, empty, empty, empty, empty, jnp.float32(0.0))
    )
    offsets = jnp.arange(1, dates_for_shard + 1, dtype=jnp.float32)[:, None, None]
    moved = shifted(tuple((part[None] for part in carried[:5])), offsets)
    zeroth, first, second, level_sum, slope_sum = (
        local[index] + moved[index] for index in range(5)
    )
    det = zeroth * (second + RIDGE) - first * first
    det = jnp.where(ocean[None] > 0, det, jnp.float32(1.0))
    slope = (first * level_sum - zeroth * slope_sum) / det
    stacked_fields = jnp.concatenate([slope, ocean[None]], axis=0)
    padded = extended(stacked_fields, (("tile", 1),), 1)
    padded = jnp.pad(padded, ((0, 0), (0, 0), (1, 1)))
    rowsum = padded[:, :-2] + padded[:, 1:-1] + padded[:, 2:]
    total = rowsum[:, :, :-2] + rowsum[:, :, 1:-1] + rowsum[:, :, 2:]
    count = jnp.maximum(total[dates_for_shard], 1.0)
    return total[:dates_for_shard] / count[None]


def solution(mesh):
    in_specs = (P("tm", "tile", None), P("tm", "tile", None), P(), P("tile", None))
    out_specs = P("tm", "tile", None)
    return jax.shard_map(
        on_device, mesh=mesh, in_specs=in_specs, out_specs=out_specs, check_vma=False
    )
```

profile of v0, /device:TPU:1, one launch (start us, length us, event | category | flops | bytes accessed | tf_op | source)
XLA Modules:
  0.0 320.2 jit_solution(12389917258836446696)
XLA Ops:
  2.0 1.8 gather_fusion
  3.8 6.4 %all-to-all-start = ((bf16[32,24,1024]{2,1,0:T(8,128)(2,1)}), bf16[32,24,1024]{2,1,0:T(8,128)(2,1)S(1)}, u32[]{:S(2)}, u32[]{:S(2)}) async-start(bf16[32,24,1024]{2,1,0:T(8,128)(2,1)} %gather_fusion), calls=%async_computation | async-start | bytes 3145728 | tf_op jit(solution)/shard_map/all_to_all | solution.py:76
  10.2 1.8 gather_fusion.1
  12.0 34.4 %all-to-all-done = bf16[32,24,1024]{2,1,0:T(8,128)(2,1)S(1)} async-done(((bf16[32,24,1024]{2,1,0:T(8,128)(2,1)}), bf16[32,24,1024]{2,1,0:T(8,128)(2,1)S(1)}, u32[]{:S(2)}, u32[]{:S(2)}) %all-to-all-start) | async-done | bytes 1572896 | tf_op jit(solution)/shard_map/all_to_all | solution.py:76
  46.4 4.6 %all-to-all-start.1 = ((bf16[32,24,1024]{2,1,0:T(8,128)(2,1)}), bf16[32,24,1024]{2,1,0:T(8,128)(2,1)S(1)}, u32[]{:S(2)}, u32[]{:S(2)}) async-start(bf16[32,24,1024]{2,1,0:T(8,128)(2,1)} %gather_fusion.1), calls=%async_computation.1 | async-start | bytes 3145728 | tf_op jit(solution)/shard_map/all_to_all | solution.py:73
  58.6 28.7 %all-to-all-done.1 = bf16[32,24,1024]{2,1,0:T(8,128)(2,1)S(1)} async-done(((bf16[32,24,1024]{2,1,0:T(8,128)(2,1)}), bf16[32,24,1024]{2,1,0:T(8,128)(2,1)S(1)}, u32[]{:S(2)}, u32[]{:S(2)}) %all-to-all-start.1) | async-done | bytes 1572896 | tf_op jit(solution)/shard_map/all_to_all | solution.py:73
  88.1 4.4 %fusion.6 = f32[64,24,1024]{2,0,1:T(8,128)S(1)} fusion(f32[32,24,1024]{2,1,0:T(8,128)S(1)} %convert_multiply_fusion, f32[32,32]{0,1:T(8,128)S(1)} %copy-done.8, f32[32,32]{0,1:T(8,128)S(1)} %copy-done.7), kind=kOutput, calls=%fused_computation.30 | convolution fusion | flops 301991936 | bytes 9445376 | tf_op jit(solution)/shard_map/ks,src->krc/dot_general | solution.py:83
  92.6 2.5 fusion.9
  95.1 3.0 convolution_add_fusion
  98.2 4.4 %slice_multiply_fusion.4 = (f32[32,24,1024]{2,0,1:T(8,128)S(1)}, f32[32,24,1024]{2,0,1:T(8,128)S(1)}, f32[32,24,1024]{2,0,1:T(8,128)}, f32[32,24,1024]{2,0,1:T(8,128)}, f32[32,24,1024]{2,0,1:T(8,128)}) fusion(f32[96,24,1024]{2,0,1:T(8,128)S(1)} %convolution_add_fusion, f32[24,1024]{1,0:T(8,128)S(1)} %copy-done.6, f32[64,24,1024]{2,0,1:T(8,128)S(1)} %fusion.6), kind=kLoop, calls=%fused_computation.29 | loop fusion | flops 3932160 | bytes 31555584 | tf_op jit(solution)/shard_map/mul | solution.py:97
  102.6 1.8 slice.88
  104.4 28.3 %all_gather.15 = f32[8,24,1024]{2,1,0:T(8,128)} all-gather(f32[1,24,1024]{2,1,0:T(8,128)S(1)} %copy.48), channel_id=1, replica_groups=mesh['tile'=4,'tm'=8] {'tm'}, dimensions={0}, use_global_device_ids=true | all-gather | bytes 884736 | tf_op jit(solution)/shard_map/all_gather | solution.py:100
  132.8 28.4 %all_gather.16 = f32[8,24,1024]{2,1,0:T(8,128)} all-gather(f32[1,24,1024]{2,1,0:T(8,128)S(1)} %copy.49), channel_id=1, replica_groups=mesh['tile'=4,'tm'=8] {'tm'}, dimensions={0}, use_global_device_ids=true | all-gather | bytes 884736 | tf_op jit(solution)/shard_map/all_gather | solution.py:101
  161.4 28.4 %all_gather.17 = f32[8,24,1024]{2,1,0:T(8,128)} all-gather(f32[1,24,1024]{2,1,0:T(8,128)S(1)} %copy.50), channel_id=1, replica_groups=mesh['tile'=4,'tm'=8] {'tm'}, dimensions={0}, use_global_device_ids=true | all-gather | bytes 884736 | tf_op jit(solution)/shard_map/all_gather | solution.py:102
  191.1 28.2 %all_gather.18 = f32[8,24,1024]{2,1,0:T(8,128)} all-gather(f32[1,24,1024]{2,1,0:T(8,128)S(1)} %copy.52), channel_id=1, replica_groups=mesh['tile'=4,'tm'=8] {'tm'}, dimensions={0}, use_global_device_ids=true | all-gather | bytes 884736 | tf_op jit(solution)/shard_map/all_gather | solution.py:103
  220.5 28.8 %all_gather.19 = f32[8,24,1024]{2,1,0:T(8,128)} all-gather(f32[1,24,1024]{2,1,0:T(8,128)S(1)} %copy.53), channel_id=1, replica_groups=mesh['tile'=4,'tm'=8] {'tm'}, dimensions={0}, use_global_device_ids=true | all-gather | bytes 884736 | tf_op jit(solution)/shard_map/all_gather | solution.py:104
  249.4 14.9 %while.22 = (s32[]{:T(128)}, f32[24,1024]{1,0:T(8,128)S(1)}, f32[24,1024]{1,0:T(8,128)S(1)}, f32[24,1024]{1,0:T(8,128)S(1)}, f32[24,1024]{1,0:T(8,128)S(1)}, /*i...) while((s32[]{:T(128)}, f32[24,1024]{1,0:T(8,128)S(1)}, ...), condition=%wide.region_2.3_spmd.clone, body=%wide.region_1.2_spmd.clone.sunk | while | flops 688132 | bytes 1474717 | solution.py:115
  249.4 1.8 fusion.31
  251.2 1.9 fusion.31
  253.1 1.9 fusion.31
  254.9 1.9 fusion.31
  256.8 1.9 fusion.31
  258.7 1.9 fusion.31
  260.5 1.9 fusion.31
  262.4 1.9 fusion.31
  264.3 6.6 %select_divide_fusion = f32[32,24,1024]{2,0,1:T(8,128)S(1)} fusion(f32[32,24,1024]{2,0,1:T(8,128)} %copy-done.2, f32[32,24,1024]{2,0,1:T(8,128)} %get-tuple-element.329, f32[32,24,1024]{2,0,1:T(8,128)} %get-tuple-element.324, f32[32,24,1024]{2,0,1:T(8,128)} %get-tuple-element.330, f32[32,24,1024]{2,0,1:T(8,128)S(1)} %get-tuple-element.322, ...), kind=kLoop, calls=%fused_computation.32 | loop fusion | flops 21233664 | bytes 19390976 | tf_op jit(solution)/shard_map/div | solution.py:125
  270.9 32.6 %collective-permute-start = (f32[33,1,1024]{2,0,1:T(8,128)S(1)}, f32[33,1,1024]{2,0,1:T(8,128)S(1)}, u32[]{:S(2)}, u32[]{:S(2)}) collective-permute-start(f32[33,1,1024]{2,0,1:T(8,128)S(1)} %get-tuple-element.327), channel_id=1, source_target_pairs={{0,8},{8,16},{16,24},{1,9},{9,17},{17,25},{2,10},{10,18},{18,26},{... | collective-permute-start | bytes 405512 | tf_op jit(solution)/shard_map/ppermute | solution.py:19
  303.5 1.9 collective-permute-start.1
  305.8 4.4 %collective-permute-done.1 = f32[33,1,1024]{2,0,1:T(8,128)S(1)} collective-permute-done((f32[33,1,1024]{2,0,1:T(8,128)S(1)}, f32[33,1,1024]{2,0,1:T(8,128)S(1)}, u32[]{:S(2)}, u32[]{:S(2)}) %collective-permute-start.1) | collective-permute-done | bytes 135200 | tf_op jit(solution)/shard_map/ppermute | solution.py:20
  310.2 3.3 %select_maximum_fusion = f32[33,26,1026]{2,0,1:T(8,128)S(1)} fusion(f32[33,1,1024]{2,0,1:T(8,128)S(1)} %collective-permute-done.1, f32[33,1,1024]{2,0,1:T(8,128)S(1)} %collective-permute-done, f32[1,24,1024]{2,0,1:T(1,128)S(1)} %copy-done.4, f32[32,24,1024]{2,0,1:T(8,128)S(1)} %select_divide_fusion), kind=kLoop, calls=%fused_computation.15 | loop fusion | flops 8803080 | bytes 7035600 | tf_op jit(solution)/shard_map/concatenate | solution.py:21
  313.8 2.1 slice_add_fusion.2
  316.7 3.5 %copy.54 = f32[32,24,1024]{2,1,0:T(8,128)} copy(f32[32,24,1024]{2,0,1:T(8,128)S(1)} %slice_divide_fusion) | data formatting | bytes 6291456 | tf_op jit(solution)/shard_map/div | solution.py:132
  (69 shorter events, 14.5 us)
Async XLA Ops:
  0.0 2.0 copy-start
  2.0 8.2 %copy-start.3 = (bf16[32,24,1024]{2,1,0:T(8,128)(2,1)S(1)}, bf16[32,24,1024]{2,1,0:T(8,128)(2,1)}, u32[]{:S(2)}) copy-start(bf16[32,24,1024]{2,1,0:T(8,128)(2,1)} %param.6) | copy-start | bytes 4718596
  3.8 42.6 %all-to-all-start = ((bf16[32,24,1024]{2,1,0:T(8,128)(2,1)}), bf16[32,24,1024]{2,1,0:T(8,128)(2,1)S(1)}, u32[]{:S(2)}, u32[]{:S(2)}) async-start(bf16[32,24,1024]{2,1,0:T(8,128)(2,1)} %gather_fusion), calls=%async_computation | async-start | bytes 3145728 | tf_op jit(solution)/shard_map/all_to_all | solution.py:76
  46.4 41.0 %all-to-all-start.1 = ((bf16[32,24,1024]{2,1,0:T(8,128)(2,1)}), bf16[32,24,1024]{2,1,0:T(8,128)(2,1)S(1)}, u32[]{:S(2)}, u32[]{:S(2)}) async-start(bf16[32,24,1024]{2,1,0:T(8,128)(2,1)} %gather_fusion.1), calls=%async_computation.1 | async-start | bytes 3145728 | tf_op jit(solution)/shard_map/all_to_all | solution.py:73
  55.1 2.0 copy-start.5
  87.4 0.7 copy-start.7
  87.4 0.7 copy-start.8
  88.1 4.4 %copy-start.9 = (f32[32,32]{0,1:T(8,128)S(1)}, f32[32,32]{0,1:T(8,128)}, u32[]{:S(2)}) copy-start(f32[32,32]{0,1:T(8,128)} %get-tuple-element.333) | copy-start | bytes 12292
  95.1 3.1 copy-start.6
  102.6 58.7 %copy-start.2 = (f32[32,24,1024]{2,0,1:T(8,128)}, f32[32,24,1024]{2,0,1:T(8,128)S(1)}, u32[]{:S(2)}) copy-start(f32[32,24,1024]{2,0,1:T(8,128)S(1)} %get-tuple-element.323) | copy-start | bytes 9437188
  249.4 14.9 %copy-start.10 = (f32[32]{0:T(128)S(1)}, f32[32]{0:T(128)}, u32[]{:S(2)}) copy-start(f32[32]{0:T(128)} %get-tuple-element.336) | copy-start | bytes 388
  249.4 14.9 %copy-start.11 = (f32[32]{0:T(128)S(1)}, f32[32]{0:T(128)}, u32[]{:S(2)}) copy-start(f32[32]{0:T(128)} %get-tuple-element.337) | copy-start | bytes 388
  264.3 6.6 %copy-start.4 = (f32[1,24,1024]{2,0,1:T(1,128)S(1)}, f32[1,24,1024]{2,0,1:T(1,128)}, u32[]{:S(2)}) copy-start(f32[1,24,1024]{2,0,1:T(1,128)} %broadcast_in_dim.25) | copy-start | bytes 294916
  270.9 34.9 %collective-permute-start = (f32[33,1,1024]{2,0,1:T(8,128)S(1)}, f32[33,1,1024]{2,0,1:T(8,128)S(1)}, u32[]{:S(2)}, u32[]{:S(2)}) collective-permute-start(f32[33,1,1024]{2,0,1:T(8,128)S(1)} %get-tuple-element.327), channel_id=1, source_target_pairs={{0,8},{8,16},{16,24},{1,9},{9,17},{17,25},{2,10},{10,18},{18,26},{... | collective-permute-start | bytes 405512 | tf_op jit(solution)/shard_map/ppermute | solution.py:19
  303.5 6.6 %collective-permute-start.1 = (f32[33,1,1024]{2,0,1:T(8,128)S(1)}, f32[33,1,1024]{2,0,1:T(8,128)S(1)}, u32[]{:S(2)}, u32[]{:S(2)}) collective-permute-start(f32[33,1,1024]{2,0,1:T(8,128)S(1)} %get-tuple-element.328), channel_id=1, source_target_pairs={{8,0},{16,8},{24,16},{9,1},{17,9},{25,17},{10,2},{18,10},{26,18},{... | collective-permute-start | bytes 405512 | tf_op jit(solution)/shard_map/ppermute | solution.py:20
  316.0 4.2 %copy-start.1 = (bf16[32,24,1024]{2,1,0:T(8,128)(2,1)S(1)}, bf16[32,24,1024]{2,1,0:T(8,128)(2,1)}, u32[]{:S(2)}) copy-start(bf16[32,24,1024]{2,1,0:T(8,128)(2,1)} %param.7) | copy-start | bytes 4718596
where the time goes:
time: 321 us; the launch traced here: 320 us
  blocking collectives  142 us (44%)
  waiting for transfers between devices  67.8 us (21%)
  starting transfers between devices  45.5 us (14%)
  other arithmetic  38.3 us (12%)
  local copies, waits for them, and re-layouts  16.1 us (5%)
  matrix products  10 us (3%)
    all_to_all x1, waiting for transfers between devices, on_device(): lax.all_to_all(sorted_quality, 'tm', split_axis=0, concat_axis=0, tiled=T...  34.4 us
    ppermute x1, starting transfers between devices, extended(): before = lax.ppermute(last, axis, up)  32.6 us
    all_gather x1, blocking collectives, on_device(): lax.all_gather(totals[4][None], 'tm', axis=0, tiled=True)  28.8 us
    all_to_all x1, waiting for transfers between devices, on_device(): lax.all_to_all(ranked_anomaly_field, 'tm', split_axis=0, concat_axis=0, t...  28.7 us
    all_gather x1, blocking collectives, on_device(): lax.all_gather(totals[2][None], 'tm', axis=0, tiled=True)  28.4 us
    all_gather x1, blocking collectives, on_device(): lax.all_gather(totals[1][None], 'tm', axis=0, tiled=True)  28.4 us
    all_gather x1, blocking collectives, on_device(): lax.all_gather(totals[0][None], 'tm', axis=0, tiled=True)  28.3 us
    all_gather x1, blocking collectives, on_device(): lax.all_gather(totals[3][None], 'tm', axis=0, tiled=True)  28.2 us
  transfers between devices with their start and end apart: 4, of which 4 were waited for; matrix products, arithmetic and copies ran while one was open for 3% of the time, Pallas kernels for 0%

commit v1 on v0

--- a/solution.py
+++ b/solution.py
@@ -7,6 +7,18 @@
 DECAY = 0.999
 UNIT = 256.0
 RIDGE = 0.05
+
+
+def in_blocks(x, dim, size):
+    lengths = x.shape
+    tiles = x.reshape(*lengths[:dim], size, lengths[dim] // size, *lengths[dim + 1 :])
+    return jnp.moveaxis(tiles, dim, 0)
+
+
+def joined_along(blocks, dim):
+    shape = list(blocks.shape[1:])
+    shape[dim] *= blocks.shape[0]
+    return jnp.moveaxis(blocks, 0, dim).reshape(shape)
 
 
 def extended(array, sides, width):
@@ -70,9 +82,16 @@
     value_kernel = jnp.concatenate([kernel_zero, kernel_one], axis=0)
     ranked_anomaly_field = ocean_heat_anomaly[shard_ranking_permutation]
     sorted_quality = observation_reliability[shard_ranking_permutation]
-    anomaly_slice = lax.all_to_all(
-        ranked_anomaly_field, "tm", split_axis=0, concat_axis=0, tiled=True
-    )
+    size, place = (lax.axis_size("tm"), lax.axis_index("tm"))
+    blocks = in_blocks(ranked_anomaly_field, 0, size)
+    finished = [blocks[place]]
+    for turn in range(1, size):
+        sent = blocks[(place + turn) % size]
+        finished.append(
+            lax.ppermute(sent, "tm", [(i_2, (i_2 + turn) % size) for i_2 in range(size)])
+        )
+    blocks = jnp.stack(finished)[(place - jnp.arange(size)) % size]
+    anomaly_slice = joined_along(blocks, 0)
     reliability_slice = lax.all_to_all(
         sorted_quality, "tm", split_axis=0, concat_axis=0, tiled=True
     )

time: 321 us -> 310 us (0.966)
  waiting for transfers between devices: 67.8 us -> 37.6 us
  local copies, waits for them, and re-layouts: 16.1 us -> 23.1 us
  blocking collectives: 142 us -> 149 us
  starting transfers between devices: 45.5 us -> 51.2 us
    all_to_all x1 -> x0, waiting for transfers between devices: 28.7 us -> none  [on_device(): lax.all_to_all(ranked_anomaly_field, 'tm', split_axis=0, concat_axis=0, t...]
    all_to_all x1, waiting for transfers between devices: 34.4 us -> 9.49 us  [on_device(): lax.all_to_all(sorted_quality, 'tm', split_axis=0, concat_axis=0, tiled=T...]
    ppermute x0 -> x7, waiting for transfers between devices: none -> 23.4 us  [on_device(): lax.ppermute(sent, 'tm', [(i_2, (i_2 + turn) % size) for i_2 in range(siz...]
    ppermute x0 -> x7, starting transfers between devices: none -> 13.3 us  [on_device(): lax.ppermute(sent, 'tm', [(i_2, (i_2 + turn) % size) for i_2 in range(siz...]
    all_gather x1, blocking collectives: 28.3 us -> 35.3 us  [on_device(): lax.all_gather(totals[0][None], 'tm', axis=0, tiled=True)]
    all_to_all x1 -> x0, starting transfers between devices: 4.63 us -> none  [on_device(): lax.all_to_all(ranked_anomaly_field, 'tm', split_axis=0, concat_axis=0, t...]
    unnamed x25 -> x39, local copies, waits for them, and re-layouts: 0.16 us -> 4.25 us
  transfers between devices with their start and end apart: 4 -> 10, of which waited for: 4 -> 6; matrix products, arithmetic and copies ran while one was open for 3% -> 5% of each run, Pallas kernels for 0% -> 0%
where the time goes in v1:
time: 310 us; the launch traced here: 309 us
  blocking collectives  149 us (48%)
  starting transfers between devices  51.2 us (17%)
  other arithmetic  37.8 us (12%)
  waiting for transfers between devices  37.6 us (12%)
  local copies, waits for them, and re-layouts  23.1 us (7%)
  matrix products  10 us (3%)
    all_gather x1, blocking collectives, on_device(): lax.all_gather(totals[0][None], 'tm', axis=0, tiled=True)  35.3 us
    ppermute x1, starting transfers between devices, extended(): before = lax.ppermute(last, axis, up)  32.2 us
    all_gather x1, blocking collectives, on_device(): lax.all_gather(totals[1][None], 'tm', axis=0, tiled=True)  29.1 us
    all_gather x1, blocking collectives, on_device(): lax.all_gather(totals[4][None], 'tm', axis=0, tiled=True)  28.9 us
    all_gather x1, blocking collectives, on_device(): lax.all_gather(totals[3][None], 'tm', axis=0, tiled=True)  28.3 us
    all_gather x1, blocking collectives, on_device(): lax.all_gather(totals[2][None], 'tm', axis=0, tiled=True)  27.6 us
    ppermute x7, waiting for transfers between devices, on_device(): lax.ppermute(sent, 'tm', [(i_2, (i_2 + turn) % size) for i_2 in range(siz...  23.4 us
    select_n x8, other arithmetic, fold_block(): jnp.where(index < me_time, new, old)  14.9 us
  transfers between devices with their start and end apart: 10, of which 6 were waited for; matrix products, arithmetic and copies ran while one was open for 5% of the time, Pallas kernels for 0%

profile of v1, /device:TPU:1, one launch (start us, length us, event | category | flops | bytes accessed | tf_op | source)
XLA Modules:
  0.0 309.3 jit_solution(8875820914899089901)
XLA Ops:
  3.9 2.1 collective-permute-start
  7.3 2.3 collective-permute-start.2
  10.5 2.4 collective-permute-start.4
  14.6 3.7 %all-to-all-start = ((bf16[32,24,1024]{2,1,0:T(8,128)(2,1)}), bf16[32,24,1024]{2,1,0:T(8,128)(2,1)S(1)}, u32[]{:S(2)}, u32[]{:S(2)}) async-start(bf16[32,24,1024]{2,1,0:T(8,128)(2,1)} %gather_fusion), calls=%async_computation | async-start | bytes 3145728 | tf_op jit(solution)/shard_map/all_to_all | solution.py:95
  25.4 3.2 %collective-permute-start.5 = (bf16[4,24,1024]{2,1,0:T(8,128)(2,1)S(1)}, bf16[4,24,1024]{2,1,0:T(8,128)(2,1)S(1)}, u32[]{:S(2)}, u32[]{:S(2)}) collective-permute-start(bf16[4,24,1024]{2,1,0:T(8,128)(2,1)S(1)} %copy-done.10), channel_id=1, source_target_pairs={{0,6},{1,7},{2,0},{3,1},{4,2},{5,3},{6,4},{7,5},{8,14},{9,15},{10,... | collective-permute-start | bytes 589832 | tf_op jit(solution)/shard_map/ppermute | solution.py:91
  34.3 18.8 %collective-permute-done.5 = bf16[4,24,1024]{2,1,0:T(8,128)(2,1)S(1)} collective-permute-done((bf16[4,24,1024]{2,1,0:T(8,128)(2,1)S(1)}, bf16[4,24,1024]{2,1,0:T(8,128)(2,1)S(1)}, u32[]{:S(2)}, u32[]{:S(2)}) %collective-permute-start.5) | collective-permute-done | bytes 196640 | tf_op jit(solution)/shard_map/ppermute | solution.py:91
  53.8 3.5 %collective-permute-done.6 = bf16[4,24,1024]{2,1,0:T(8,128)(2,1)S(1)} collective-permute-done((bf16[4,24,1024]{2,1,0:T(8,128)(2,1)S(1)}, bf16[4,24,1024]{2,1,0:T(8,128)(2,1)S(1)}, u32[]{:S(2)}, u32[]{:S(2)}) %collective-permute-start.6) | collective-permute-done | bytes 196640 | tf_op jit(solution)/shard_map/ppermute | solution.py:91
  58.0 2.2 gather_fusion.2
  60.2 9.5 %all-to-all-done = bf16[32,24,1024]{2,1,0:T(8,128)(2,1)S(1)} async-done(((bf16[32,24,1024]{2,1,0:T(8,128)(2,1)}), bf16[32,24,1024]{2,1,0:T(8,128)(2,1)S(1)}, u32[]{:S(2)}, u32[]{:S(2)}) %all-to-all-start) | async-done | bytes 1572896 | tf_op jit(solution)/shard_map/all_to_all | solution.py:95
  70.4 4.4 %fusion.6 = f32[64,24,1024]{2,0,1:T(8,128)S(1)} fusion(f32[32,24,1024]{2,1,0:T(8,128)S(1)} %convert_multiply_fusion, f32[32,32]{0,1:T(8,128)S(1)} %copy-done.8, f32[32,32]{0,1:T(8,128)S(1)} %get-tuple-element.339), kind=kOutput, calls=%fused_computation.32 | convolution fusion | flops 301991936 | bytes 9445376 | tf_op jit(solution)/shard_map/ks,src->krc/dot_general | solution.py:102
  74.9 2.5 fusion.9
  77.4 3.1 convolution_add_fusion
  80.5 4.4 %slice_multiply_fusion.4 = (f32[32,24,1024]{2,0,1:T(8,128)S(1)}, f32[32,24,1024]{2,0,1:T(8,128)S(1)}, f32[32,24,1024]{2,0,1:T(8,128)}, f32[32,24,1024]{2,0,1:T(8,128)}, f32[32,24,1024]{2,0,1:T(8,128)}) fusion(f32[96,24,1024]{2,0,1:T(8,128)S(1)} %convolution_add_fusion, f32[24,1024]{1,0:T(8,128)S(1)} %copy-done.6, f32[64,24,1024]{2,0,1:T(8,128)S(1)} %fusion.6), kind=kLoop, calls=%fused_computation.30 | loop fusion | flops 3932160 | bytes 31555584 | tf_op jit(solution)/shard_map/mul | solution.py:116
  86.8 35.3 %all_gather.15 = f32[8,24,1024]{2,1,0:T(8,128)} all-gather(f32[1,24,1024]{2,1,0:T(8,128)S(1)} %copy.48), channel_id=1, replica_groups=mesh['tile'=4,'tm'=8] {'tm'}, dimensions={0}, use_global_device_ids=true | all-gather | bytes 884736 | tf_op jit(solution)/shard_map/all_gather | solution.py:119
  122.1 29.1 %all_gather.16 = f32[8,24,1024]{2,1,0:T(8,128)} all-gather(f32[1,24,1024]{2,1,0:T(8,128)S(1)} %copy.49), channel_id=1, replica_groups=mesh['tile'=4,'tm'=8] {'tm'}, dimensions={0}, use_global_device_ids=true | all-gather | bytes 884736 | tf_op jit(solution)/shard_map/all_gather | solution.py:120
  151.4 27.6 %all_gather.17 = f32[8,24,1024]{2,1,0:T(8,128)} all-gather(f32[1,24,1024]{2,1,0:T(8,128)S(1)} %copy.50), channel_id=1, replica_groups=mesh['tile'=4,'tm'=8] {'tm'}, dimensions={0}, use_global_device_ids=true | all-gather | bytes 884736 | tf_op jit(solution)/shard_map/all_gather | solution.py:121
  180.2 28.3 %all_gather.18 = f32[8,24,1024]{2,1,0:T(8,128)} all-gather(f32[1,24,1024]{2,1,0:T(8,128)S(1)} %copy.52), channel_id=1, replica_groups=mesh['tile'=4,'tm'=8] {'tm'}, dimensions={0}, use_global_device_ids=true | all-gather | bytes 884736 | tf_op jit(solution)/shard_map/all_gather | solution.py:122
  209.8 28.9 %all_gather.19 = f32[8,24,1024]{2,1,0:T(8,128)} all-gather(f32[1,24,1024]{2,1,0:T(8,128)S(1)} %copy.53), channel_id=1, replica_groups=mesh['tile'=4,'tm'=8] {'tm'}, dimensions={0}, use_global_device_ids=true | all-gather | bytes 884736 | tf_op jit(solution)/shard_map/all_gather | solution.py:123
  238.7 15.0 %while.22 = (s32[]{:T(128)}, f32[24,1024]{1,0:T(8,128)S(1)}, f32[24,1024]{1,0:T(8,128)S(1)}, f32[24,1024]{1,0:T(8,128)S(1)}, f32[24,1024]{1,0:T(8,128)S(1)}, /*i...) while((s32[]{:T(128)}, f32[24,1024]{1,0:T(8,128)S(1)}, ...), condition=%wide.region_2.3_spmd.clone, body=%wide.region_1.2_spmd.clone.sunk | while | flops 688132 | bytes 1474717 | solution.py:134
  240.6 1.9 fusion.34
  242.4 1.9 fusion.34
  244.3 1.9 fusion.34
  246.2 1.9 fusion.34
  248.1 1.9 fusion.34
  249.9 1.9 fusion.34
  253.7 6.6 %select_divide_fusion = f32[32,24,1024]{2,0,1:T(8,128)S(1)} fusion(f32[32,24,1024]{2,0,1:T(8,128)} %copy-done.2, f32[32,24,1024]{2,0,1:T(8,128)} %get-tuple-element.337, f32[32,24,1024]{2,0,1:T(8,128)} %get-tuple-element.324, f32[32,24,1024]{2,0,1:T(8,128)} %get-tuple-element.338, f32[32,24,1024]{2,0,1:T(8,128)S(1)} %get-tuple-element.322, ...), kind=kLoop, calls=%fused_computation.34 | loop fusion | flops 21233664 | bytes 19390976 | tf_op jit(solution)/shard_map/div | solution.py:144
  260.3 32.2 %collective-permute-start.7 = (f32[33,1,1024]{2,0,1:T(8,128)S(1)}, f32[33,1,1024]{2,0,1:T(8,128)S(1)}, u32[]{:S(2)}, u32[]{:S(2)}) collective-permute-start(f32[33,1,1024]{2,0,1:T(8,128)S(1)} %get-tuple-element.327), channel_id=1, source_target_pairs={{0,8},{8,16},{16,24},{1,9},{9,17},{17,25},{2,10},{10,18},{18,26},{... | collective-permute-start | bytes 405512 | tf_op jit(solution)/shard_map/ppermute | solution.py:31
  292.6 1.9 collective-permute-start.8
  294.8 4.4 %collective-permute-done.8 = f32[33,1,1024]{2,0,1:T(8,128)S(1)} collective-permute-done((f32[33,1,1024]{2,0,1:T(8,128)S(1)}, f32[33,1,1024]{2,0,1:T(8,128)S(1)}, u32[]{:S(2)}, u32[]{:S(2)}) %collective-permute-start.8) | collective-permute-done | bytes 135200 | tf_op jit(solution)/shard_map/ppermute | solution.py:32
  299.2 3.3 %select_maximum_fusion = f32[33,26,1026]{2,0,1:T(8,128)S(1)} fusion(f32[33,1,1024]{2,0,1:T(8,128)S(1)} %collective-permute-done.8, f32[33,1,1024]{2,0,1:T(8,128)S(1)} %collective-permute-done.7, f32[1,24,1024]{2,0,1:T(1,128)S(1)} %copy-done.4, f32[32,24,1024]{2,0,1:T(8,128)S(1)} %select_divide_fusion), kind=kLoop, calls=%fused_computation.16 | loop fusion | flops 8803080 | bytes 7035600 | tf_op jit(solution)/shard_map/concatenate | solution.py:33
  302.9 2.1 slice_add_fusion.2
  305.8 3.5 %copy.54 = f32[32,24,1024]{2,1,0:T(8,128)} copy(f32[32,24,1024]{2,0,1:T(8,128)S(1)} %slice_divide_fusion) | data formatting | bytes 6291456 | tf_op jit(solution)/shard_map/div | solution.py:151
  (100 shorter events, 32.4 us)
Async XLA Ops:
  0.0 2.0 copy-start
  2.7 10.1 %copy-start.3 = (bf16[32,24,1024]{2,1,0:T(8,128)(2,1)S(1)}, bf16[32,24,1024]{2,1,0:T(8,128)(2,1)}, u32[]{:S(2)}) copy-start(bf16[32,24,1024]{2,1,0:T(8,128)(2,1)} %param.7) | copy-start | bytes 4718596
  3.9 21.5 %collective-permute-start = (bf16[4,24,1024]{2,1,0:T(8,128)(2,1)}, bf16[4,24,1024]{2,1,0:T(8,128)(2,1)S(1)}, u32[]{:S(2)}, u32[]{:S(2)}) collective-permute-start(bf16[4,24,1024]{2,1,0:T(8,128)(2,1)} %get-tuple-element.335), channel_id=1, source_target_pairs={{0,1},{1,2},{2,3},{3,4},{4,5},{5,6},{6,7},{7,0},{8,9},{9,10},{10,1... | collective-permute-start | bytes 589832 | tf_op jit(solution)/shard_map/ppermute | solution.py:91
  6.0 23.3 %collective-permute-start.1 = (bf16[4,24,1024]{2,1,0:T(8,128)(2,1)}, bf16[4,24,1024]{2,1,0:T(8,128)(2,1)S(1)}, u32[]{:S(2)}, u32[]{:S(2)}) collective-permute-start(bf16[4,24,1024]{2,1,0:T(8,128)(2,1)} %get-tuple-element.334), channel_id=1, source_target_pairs={{0,2},{1,3},{2,4},{3,5},{4,6},{5,7},{6,0},{7,1},{8,10},{9,11},{10,... | collective-permute-start | bytes 589832 | tf_op jit(solution)/shard_map/ppermute | solution.py:91
  7.3 25.0 %collective-permute-start.2 = (bf16[4,24,1024]{2,1,0:T(8,128)(2,1)}, bf16[4,24,1024]{2,1,0:T(8,128)(2,1)S(1)}, u32[]{:S(2)}, u32[]{:S(2)}) collective-permute-start(bf16[4,24,1024]{2,1,0:T(8,128)(2,1)} %get-tuple-element.333), channel_id=1, source_target_pairs={{0,3},{1,4},{2,5},{3,6},{4,7},{5,0},{6,1},{7,2},{8,11},{9,12},{10,... | collective-permute-start | bytes 589832 | tf_op jit(solution)/shard_map/ppermute | solution.py:91
  9.5 23.4 %collective-permute-start.3 = (bf16[4,24,1024]{2,1,0:T(8,128)(2,1)}, bf16[4,24,1024]{2,1,0:T(8,128)(2,1)S(1)}, u32[]{:S(2)}, u32[]{:S(2)}) collective-permute-start(bf16[4,24,1024]{2,1,0:T(8,128)(2,1)} %get-tuple-element.332), channel_id=1, source_target_pairs={{0,4},{1,5},{2,6},{3,7},{4,0},{5,1},{6,2},{7,3},{8,12},{9,13},{10,... | collective-permute-start | bytes 589832 | tf_op jit(solution)/shard_map/ppermute | solution.py:91
  10.5 23.1 %collective-permute-start.4 = (bf16[4,24,1024]{2,1,0:T(8,128)(2,1)}, bf16[4,24,1024]{2,1,0:T(8,128)(2,1)S(1)}, u32[]{:S(2)}, u32[]{:S(2)}) collective-permute-start(bf16[4,24,1024]{2,1,0:T(8,128)(2,1)} %get-tuple-element.331), channel_id=1, source_target_pairs={{0,5},{1,6},{2,7},{3,0},{4,1},{5,2},{6,3},{7,4},{8,13},{9,14},{10,... | collective-permute-start | bytes 589832 | tf_op jit(solution)/shard_map/ppermute | solution.py:91
  14.6 6.3 %copy-start.7 = (s32[24,1024]{1,0:T(8,128)S(1)}, s32[24,1024]{1,0:T(8,128)}, u32[]{:S(2)}) copy-start(s32[24,1024]{1,0:T(8,128)} %param.9) | copy-start | bytes 294916
  14.6 55.0 %all-to-all-start = ((bf16[32,24,1024]{2,1,0:T(8,128)(2,1)}), bf16[32,24,1024]{2,1,0:T(8,128)(2,1)S(1)}, u32[]{:S(2)}, u32[]{:S(2)}) async-start(bf16[32,24,1024]{2,1,0:T(8,128)(2,1)} %gather_fusion), calls=%async_computation | async-start | bytes 3145728 | tf_op jit(solution)/shard_map/all_to_all | solution.py:95
  18.3 7.0 %copy-start.10 = (bf16[4,24,1024]{2,1,0:T(8,128)(2,1)S(1)}, bf16[4,24,1024]{2,1,0:T(8,128)(2,1)}, u32[]{:S(2)}) copy-start(bf16[4,24,1024]{2,1,0:T(8,128)(2,1)} %get-tuple-element.330) | copy-start | bytes 589828
  18.4 10.9 %copy-start.9 = (bf16[4,24,1024]{2,1,0:T(8,128)(2,1)S(1)}, bf16[4,24,1024]{2,1,0:T(8,128)(2,1)}, u32[]{:S(2)}) copy-start(bf16[4,24,1024]{2,1,0:T(8,128)(2,1)} %get-tuple-element.329) | copy-start | bytes 589828
  20.9 36.4 %copy-start.5 = (f32[24,1024]{1,0:T(8,128)}, f32[24,1024]{1,0:T(8,128)S(1)}, u32[]{:S(2)}) copy-start(f32[24,1024]{1,0:T(8,128)S(1)} %convert_element_type.30) | copy-start | bytes 294916
  25.4 27.7 %collective-permute-start.5 = (bf16[4,24,1024]{2,1,0:T(8,128)(2,1)S(1)}, bf16[4,24,1024]{2,1,0:T(8,128)(2,1)S(1)}, u32[]{:S(2)}, u32[]{:S(2)}) collective-permute-start(bf16[4,24,1024]{2,1,0:T(8,128)(2,1)S(1)} %copy-done.10), channel_id=1, source_target_pairs={{0,6},{1,7},{2,0},{3,1},{4,2},{5,3},{6,4},{7,5},{8,14},{9,15},{10,... | collective-permute-start | bytes 589832 | tf_op jit(solution)/shard_map/ppermute | solution.py:91
  29.3 28.0 %collective-permute-start.6 = (bf16[4,24,1024]{2,1,0:T(8,128)(2,1)S(1)}, bf16[4,24,1024]{2,1,0:T(8,128)(2,1)S(1)}, u32[]{:S(2)}, u32[]{:S(2)}) collective-permute-start(bf16[4,24,1024]{2,1,0:T(8,128)(2,1)S(1)} %copy-done.9), channel_id=1, source_target_pairs={{0,7},{1,0},{2,1},{3,2},{4,3},{5,4},{6,5},{7,6},{8,15},{9,8},{10,9... | collective-permute-start | bytes 589832 | tf_op jit(solution)/shard_map/ppermute | solution.py:91
  69.7 0.7 copy-start.8
  70.4 4.5 %copy-start.11 = (f32[32,32]{0,1:T(8,128)S(1)}, f32[32,32]{0,1:T(8,128)}, u32[]{:S(2)}) copy-start(f32[32,32]{0,1:T(8,128)} %get-tuple-element.341) | copy-start | bytes 12292
  77.4 3.1 copy-start.6
  84.9 66.3 %copy-start.2 = (f32[32,24,1024]{2,0,1:T(8,128)}, f32[32,24,1024]{2,0,1:T(8,128)S(1)}, u32[]{:S(2)}) copy-start(f32[32,24,1024]{2,0,1:T(8,128)S(1)} %get-tuple-element.323) | copy-start | bytes 9437188
  238.7 15.0 %copy-start.12 = (f32[32]{0:T(128)S(1)}, f32[32]{0:T(128)}, u32[]{:S(2)}) copy-start(f32[32]{0:T(128)} %get-tuple-element.342) | copy-start | bytes 388
  238.7 15.0 %copy-start.13 = (f32[32]{0:T(128)S(1)}, f32[32]{0:T(128)}, u32[]{:S(2)}) copy-start(f32[32]{0:T(128)} %get-tuple-element.343) | copy-start | bytes 388
  238.7 15.0 %copy-start.14 = (f32[32]{0:T(128)S(1)}, f32[32]{0:T(128)}, u32[]{:S(2)}) copy-start(f32[32]{0:T(128)} %get-tuple-element.344) | copy-start | bytes 388
  238.7 15.0 %copy-start.15 = (f32[32]{0:T(128)S(1)}, f32[32]{0:T(128)}, u32[]{:S(2)}) copy-start(f32[32]{0:T(128)} %get-tuple-element.345) | copy-start | bytes 388
  253.7 6.6 %copy-start.4 = (f32[1,24,1024]{2,0,1:T(1,128)S(1)}, f32[1,24,1024]{2,0,1:T(1,128)}, u32[]{:S(2)}) copy-start(f32[1,24,1024]{2,0,1:T(1,128)} %broadcast_in_dim.25) | copy-start | bytes 294916
  260.3 34.5 %collective-permute-start.7 = (f32[33,1,1024]{2,0,1:T(8,128)S(1)}, f32[33,1,1024]{2,0,1:T(8,128)S(1)}, u32[]{:S(2)}, u32[]{:S(2)}) collective-permute-start(f32[33,1,1024]{2,0,1:T(8,128)S(1)} %get-tuple-element.327), channel_id=1, source_target_pairs={{0,8},{8,16},{16,24},{1,9},{9,17},{17,25},{2,10},{10,18},{18,26},{... | collective-permute-start | bytes 405512 | tf_op jit(solution)/shard_map/ppermute | solution.py:31
  292.6 6.6 %collective-permute-start.8 = (f32[33,1,1024]{2,0,1:T(8,128)S(1)}, f32[33,1,1024]{2,0,1:T(8,128)S(1)}, u32[]{:S(2)}, u32[]{:S(2)}) collective-permute-start(f32[33,1,1024]{2,0,1:T(8,128)S(1)} %get-tuple-element.328), channel_id=1, source_target_pairs={{8,0},{16,8},{24,16},{9,1},{17,9},{25,17},{10,2},{18,10},{26,18},{... | collective-permute-start | bytes 405512 | tf_op jit(solution)/shard_map/ppermute | solution.py:32
  305.1 4.2 %copy-start.1 = (bf16[32,24,1024]{2,1,0:T(8,128)(2,1)S(1)}, bf16[32,24,1024]{2,1,0:T(8,128)(2,1)}, u32[]{:S(2)}) copy-start(bf16[32,24,1024]{2,1,0:T(8,128)(2,1)} %param.6) | copy-start | bytes 4718596
